TPU v7x, 32 devices: a whole 2x2x4 slice. The times are simulated.
32 devices in a mesh: rcp: 4 (over y, x), lon: 8 (over z, core).
Axes of the slice: x: 2, y: 2, z: 4, core: 2. Of those that a mesh axis runs over, the one named last changes fastest.
Arguments:
- adj_in: float32 [32, 32, 128, 128], P('rcp', None, 'lon'), may hold values from -6 to 6
- mass_flux: float32 [4, 2, 6, 32, 128, 128], P('rcp', None, None, None, 'lon'), may hold values from -0.24 to 0.24
- mixing: float32 [4, 128, 32, 32], P('rcp', 'lon'), may hold values from 0 to 0.7, as said below
- window_owner: int32 [6], replicated, may hold values from 0 to 3
- receptor_lon: int32 [32], P('rcp'), may hold values from 0 to 127
- receptor_lat: int32 [32], P('rcp'), may hold values from 0 to 127
- release_step: int32 [32], P('rcp'), may hold values from 0 to 5
Outputs:
- adj_out: float32 [32, 32, 128, 128], P('rcp', None, 'lon')
- footprint: float32 [32, 128, 128], P('rcp', 'lon')
Inputs may be any that keep to these rules, and one draw needn't show every extreme that they name: `mixing`: every entry is non-negative.
All inputs are finite; a program needn't handle non-finite values.
Results may differ from a plain program's by a relative error of at most 0.0003.
Values sent between devices are 32-bit elements; how exact they have to be, the bound alone decides.
No kernel may reach another device: no remote copies, remote signals or barrier semaphores. Data moves between devices by JAX's collectives and lax.ppermute only.
A program may use at most 128 MiB of HBM per device.

v0:
```python
import jax
import jax.numpy as jnp
from jax import lax
from jax.sharding import PartitionSpec as P

STEPS = 6


def from_root(block, axis, owner):
    block = jnp.where(lax.axis_index(axis) == owner, block, jnp.zeros_like(block))
    return lax.psum(block, axis)


def shifted(block, axis, distance):
    devices = range(lax.axis_size(axis))
    route = [((i - distance) % len(devices), i) for i in devices]
    return lax.ppermute(block, axis, route)


def padded_2(block, sides, width):
    for axis, dim in sides:
        count = lax.axis_size(axis)
        forward = [(i, i + 1) for i in range(count - 1)]
        forward.append((count - 1, 0))
        backward = [(target, source) for source, target in forward]
        low = lax.ppermute(
            lax.slice_in_dim(block, block.shape[dim] - width, None, axis=dim), axis, forward
        )
        high = lax.ppermute(lax.slice_in_dim(block, 0, width, axis=dim), axis, backward)
        block = jnp.concatenate([low, block, high], axis=dim)
    return block


def inject(field, columns, step, rlon, rlat, rel):
    lats = jnp.arange(field.shape[3], dtype=jnp.int32)
    hit = (
        (columns[None, :, None] == rlon[:, None, None])
        & (lats[None, None, :] == rlat[:, None, None])
        & (rel[:, None, None] == step)
    )
    return field.at[:, 0].add(hit.astype(jnp.float32))


def advance(padded, u_west, u_east, v_south, mats):
    centre = padded[:, :, 1:-1]
    left = padded[:, :, :-2]
    right = padded[:, :, 2:]
    west = jnp.maximum(u_west, 0.0) * left + jnp.minimum(u_west, 0.0) * centre
    east = jnp.maximum(u_east, 0.0) * centre + jnp.minimum(u_east, 0.0) * right
    lat_index = lax.broadcasted_iota(jnp.int32, v_south.shape, 2)
    vs = jnp.where(lat_index > 0, v_south, jnp.float32(0.0))
    vn = jnp.concatenate([vs[:, :, 1:], jnp.zeros_like(vs[:, :, :1])], axis=2)
    below = jnp.concatenate([jnp.zeros_like(centre[..., :1]), centre[..., :-1]], axis=3)
    above = jnp.concatenate([centre[..., 1:], jnp.zeros_like(centre[..., :1])], axis=3)
    south = jnp.maximum(vs, 0.0) * below + jnp.minimum(vs, 0.0) * centre
    north = jnp.maximum(vn, 0.0) * centre + jnp.minimum(vn, 0.0) * above
    moved = centre + west - east + south - north
    return jnp.einsum(
        "kab,rbky->raky",
        mats,
        moved,
        precision=lax.Precision.HIGHEST,
        preferred_element_type=jnp.float32,
    )


def local(adj_in, mass_flux, mixing, window_owner, receptor_lon, receptor_lat, release_step):
    flux_steps = []
    mat_steps = []
    for step in range(STEPS):
        flux_step, mats_step = (
            from_root(mass_flux[:, :, step], "rcp", window_owner[step]),
            from_root(mixing, "rcp", window_owner[step]),
        )
        flux_steps.append(flux_step[0])
        mat_steps.append(mats_step[0])
    flux = jnp.stack(flux_steps, axis=1)
    mats = jnp.stack(mat_steps, axis=0)
    width = adj_in.shape[2]
    start = lax.axis_index("lon") * width
    field = adj_in
    footprint = jnp.zeros((adj_in.shape[0], width, adj_in.shape[3]), jnp.float32)
    columns = start + jnp.arange(width, dtype=jnp.int32)
    edge = shifted(flux[0, :, :, 0:1, :], "lon", -1)
    east_all = jnp.concatenate([flux[0, :, :, 1:], edge], axis=2)
    for step in range(STEPS):
        field = inject(field, columns, step, receptor_lon, receptor_lat, release_step)
        padded = padded_2(field, (("lon", 2),), 1)
        field = advance(padded, flux[0, step], east_all[step], flux[1, step], mats[step])
        footprint = footprint + field[:, 0]
    return (field, footprint)


def solution(mesh):
    return jax.shard_map(
        local,
        mesh=mesh,
        in_specs=(
            P("rcp", None, "lon", None),
            P("rcp", None, None, None, "lon", None),
            P("rcp", "lon", None, None),
            P(),
            P("rcp"),
            P("rcp"),
            P("rcp"),
        ),
        out_specs=(P("rcp", None, "lon", None), P("rcp", "lon", None)),
        check_vma=False,
    )
```

profile of v0, /device:TPU:0, one launch (start us, length us, event | category | flops | bytes accessed | tf_op | source)
XLA Modules:
  0.0 259.6 jit_solution(11546297863126476404)
XLA Ops:
  12.6 1.9 fusion.173
  14.5 3.3 %fusion.168 = (f32[1,2,32,16,128]{4,3,2,1,0:T(8,128)}, f32[1,2,32,16,128]{4,3,2,1,0:T(8,128)}, f32[1,2,32,16,128]{4,3,2,1,0:T(8,128)}, f32[1,2,32,16,128]{4,3,2,1,0:T(8,128)}, f32[1,2,32,16,128]{4,3,2,1,0:T(8,128)}) fusion(f32[1,2,6,32,16,128]{5,4,3,2,1,0:T(8,128)} %param.20, pred[]{:T(512)S(6)} %eq.64, pred[]{:T(512)S(6)} %eq.63, pred[]{:T(512)S(6)} %eq.61, ...), kind=kLoop, calls=%fused_computation.180 | loop fusion | flops 655360 | bytes 5242885 | tf_op jit(solution)/shard_map/jit(_where)/select_n | solution.py:10
  19.1 2.3 copy.62
  24.5 4.0 %collective-permute-start.2 = (f32[8,32,1,128]{3,1,2,0:T(8,128)}, f32[8,32,1,128]{3,1,2,0:T(8,128)}, u32[]{:S(2)}, u32[]{:S(2)}) collective-permute-start(f32[8,32,1,128]{3,1,2,0:T(8,128)} %get-tuple-element.132), channel_id=1, source_target_pairs={{1,0},{2,1},{3,2},{4,3},{5,4},{6,5},{7,6},{0,7},{9,8},{10,9},{11,1... | collective-permute-start | bytes 393224 | tf_op jit(solution)/shard_map/ppermute | solution.py:29
  28.5 2.8 %fusion.229 = (f32[8,32,16,127]{3,1,2,0:T(8,128)}, f32[8,32,16,127]{3,1,2,0:T(8,128)}) fusion(f32[8,32,16,128]{3,1,2,0:T(8,128)S(1)} %scatter-add.20), kind=kLoop, calls=%fused_computation.333 | loop fusion | bytes 8323072 | tf_op jit(solution)/shard_map/slice | solution.py:53
  31.3 103.5 %all-reduce.21.cloned.1.call-done = (f32[1,2,32,16,128]{4,3,2,1,0:T(8,128)}, f32[1,2,32,16,128]{4,3,2,1,0:T(8,128)}, f32[1,2,32,16,128]{4,3,2,1,0:T(8,128)}, f32...) async-done(((f32[1,2,32,16,128]{4,3,2,1,0:T(8,128)}, ...) | async-done | bytes 3538960 | tf_op jit(solution)/shard_map/psum | solution.py:11
  140.2 3.2 %collective-permute-start.1 = (f32[6,32,1,128]{3,1,0,2:T(8,128)S(1)}, f32[6,32,1,128]{3,1,0,2:T(8,128)S(1)}, u32[]{:S(2)}, u32[]{:S(2)}) collective-permute-start(f32[6,32,1,128]{3,1,0,2:T(8,128)S(1)} %bitcast.219), channel_id=1, source_target_pairs={{1,0},{2,1},{3,2},{4,3},{5,4},{6,5},{7,6},{0,7},{9,8},{10,9},{11,1... | collective-permute-start | bytes 294920 | tf_op jit(solution)/shard_map/ppermute | solution.py:17
  170.4 4.4 %fusion.73 = f32[16,8,128,32]{2,3,1,0:T(8,128)S(1)} fusion(f32[16,32,32]{2,1,0:T(8,128)S(1)} %copy-done.60, f32[8,32,1,128]{3,1,2,0:T(8,128)} %collective-permute-done.2, f32[8,32,16,128]{3,1,2,0:T(8,128)S(1)} %scatter-add.20, f32[8,32,1,128]{3,1,2,0:T(8,128)} %collective-permute-done, f32[8,32,16,127]{3,1,2,0:T(8,128)S(1)} %copy-done.14, ...), kind=kOutput, calls=%fused_computation.80 | convolution fusion | flops 210763776 | bytes 10780672 | tf_op jit(solution)/shard_map/kab,rbky->raky/dot_general | solution.py:58
  177.0 2.0 scatter-add.21
  180.5 3.7 %collective-permute-start.4 = (f32[8,32,1,128]{3,1,0,2:T(8,128)S(1)}, f32[8,32,1,128]{3,1,0,2:T(8,128)S(1)}, u32[]{:S(2)}, u32[]{:S(2)}) collective-permute-start(f32[8,32,1,128]{3,1,0,2:T(8,128)S(1)} %get-tuple-element.128), channel_id=1, source_target_pairs={{1,0},{2,1},{3,2},{4,3},{5,4},{6,5},{7,6},{0,7},{9,8},{10,9},{11,1... | collective-permute-start | bytes 393224 | tf_op jit(solution)/shard_map/ppermute | solution.py:29
  188.1 3.4 %fusion.57 = f32[16,8,128,32]{2,3,1,0:T(8,128)S(1)} fusion(f32[8,32,1,128]{3,1,0,2:T(8,128)S(1)} %collective-permute-done.4, f32[8,32,16,128]{3,1,0,2:T(8,128)S(1)} %scatter-add.21, f32[8,32,1,128]{3,1,0,2:T(8,128)S(1)} %collective-permute-done.3, f32[8,32,16,127]{3,1,0,2:T(8,128)S(1)} %get-tuple-element.126, ...), kind=kOutput, calls=%fused_computation.63 | convolution fusion | flops 210763776 | bytes 10780672 | tf_op jit(solution)/shard_map/kab,rbky->raky/dot_general | solution.py:58
  194.6 3.6 %collective-permute-start.6 = (f32[8,32,1,128]{3,1,0,2:T(8,128)S(1)}, f32[8,32,1,128]{3,1,0,2:T(8,128)S(1)}, u32[]{:S(2)}, u32[]{:S(2)}) collective-permute-start(f32[8,32,1,128]{3,1,0,2:T(8,128)S(1)} %get-tuple-element.124), channel_id=1, source_target_pairs={{1,0},{2,1},{3,2},{4,3},{5,4},{6,5},{7,6},{0,7},{9,8},{10,9},{11,1... | collective-permute-start | bytes 393224 | tf_op jit(solution)/shard_map/ppermute | solution.py:29
  198.9 2.8 %collective-permute-done.5 = f32[8,32,1,128]{3,1,0,2:T(8,128)S(1)} collective-permute-done((f32[8,32,1,128]{3,1,0,2:T(8,128)S(1)}, f32[8,32,1,128]{3,1,0,2:T(8,128)S(1)}, u32[]{:S(2)}, u32[]{:S(2)}) %collective-permute-start.5) | collective-permute-done | bytes 131104 | tf_op jit(solution)/shard_map/ppermute | solution.py:26
  201.8 3.4 %fusion.44 = f32[16,8,128,32]{2,3,1,0:T(8,128)S(1)} fusion(f32[8,32,1,128]{3,1,0,2:T(8,128)S(1)} %collective-permute-done.6, f32[8,32,16,128]{3,1,0,2:T(8,128)S(1)} %scatter-add.24, f32[8,32,1,128]{3,1,0,2:T(8,128)S(1)} %collective-permute-done.5, f32[8,32,16,127]{3,1,0,2:T(8,128)S(1)} %get-tuple-element.122, ...), kind=kOutput, calls=%fused_computation.50 | convolution fusion | flops 210763776 | bytes 10780672 | tf_op jit(solution)/shard_map/kab,rbky->raky/dot_general | solution.py:58
  208.3 3.8 %collective-permute-start.8 = (f32[8,32,1,128]{3,1,0,2:T(8,128)S(1)}, f32[8,32,1,128]{3,1,0,2:T(8,128)S(1)}, u32[]{:S(2)}, u32[]{:S(2)}) collective-permute-start(f32[8,32,1,128]{3,1,0,2:T(8,128)S(1)} %get-tuple-element.120), channel_id=1, source_target_pairs={{1,0},{2,1},{3,2},{4,3},{5,4},{6,5},{7,6},{0,7},{9,8},{10,9},{11,1... | collective-permute-start | bytes 393224 | tf_op jit(solution)/shard_map/ppermute | solution.py:29
  212.8 2.9 %collective-permute-done.7 = f32[8,32,1,128]{3,1,0,2:T(8,128)S(1)} collective-permute-done((f32[8,32,1,128]{3,1,0,2:T(8,128)S(1)}, f32[8,32,1,128]{3,1,0,2:T(8,128)S(1)}, u32[]{:S(2)}, u32[]{:S(2)}) %collective-permute-start.7) | collective-permute-done | bytes 131104 | tf_op jit(solution)/shard_map/ppermute | solution.py:26
  215.8 3.4 %fusion.31 = f32[16,8,128,32]{2,3,1,0:T(8,128)S(1)} fusion(f32[8,32,1,128]{3,1,0,2:T(8,128)S(1)} %collective-permute-done.8, f32[8,32,16,128]{3,1,0,2:T(8,128)S(1)} %scatter-add.25, f32[8,32,1,128]{3,1,0,2:T(8,128)S(1)} %collective-permute-done.7, f32[8,32,16,127]{3,1,0,2:T(8,128)S(1)} %get-tuple-element.118, ...), kind=kOutput, calls=%fused_computation.37 | convolution fusion | flops 210763776 | bytes 10780672 | tf_op jit(solution)/shard_map/kab,rbky->raky/dot_general | solution.py:58
  222.2 2.6 %collective-permute-start.10 = (f32[8,32,1,128]{3,1,0,2:T(8,128)S(1)}, f32[8,32,1,128]{3,1,0,2:T(8,128)S(1)}, u32[]{:S(2)}, u32[]{:S(2)}) collective-permute-start(f32[8,32,1,128]{3,1,0,2:T(8,128)S(1)} %get-tuple-element.116), channel_id=1, source_target_pairs={{1,0},{2,1},{3,2},{4,3},{5,4},{6,5},{7,6},{0,7},{9,8},{10,9},{11,1... | collective-permute-start | bytes 393224 | tf_op jit(solution)/shard_map/ppermute | solution.py:29
  227.3 3.8 %collective-permute-done.9 = f32[8,32,1,128]{3,1,0,2:T(8,128)S(1)} collective-permute-done((f32[8,32,1,128]{3,1,0,2:T(8,128)S(1)}, f32[8,32,1,128]{3,1,0,2:T(8,128)S(1)}, u32[]{:S(2)}, u32[]{:S(2)}) %collective-permute-start.9) | collective-permute-done | bytes 131104 | tf_op jit(solution)/shard_map/ppermute | solution.py:26
  231.1 3.4 %fusion.18 = f32[16,8,128,32]{2,3,1,0:T(8,128)S(1)} fusion(f32[8,32,1,128]{3,1,0,2:T(8,128)S(1)} %collective-permute-done.10, f32[8,32,16,128]{3,1,0,2:T(8,128)S(1)} %scatter-add.26, f32[8,32,1,128]{3,1,0,2:T(8,128)S(1)} %collective-permute-done.9, f32[8,32,16,127]{3,1,0,2:T(8,128)S(1)} %get-tuple-element.114, ...), kind=kOutput, calls=%fused_computation.24 | convolution fusion | flops 210763776 | bytes 10780672 | tf_op jit(solution)/shard_map/kab,rbky->raky/dot_general | solution.py:58
  237.6 3.8 %collective-permute-start.12 = (f32[8,32,1,128]{3,1,0,2:T(8,128)S(1)}, f32[8,32,1,128]{3,1,0,2:T(8,128)S(1)}, u32[]{:S(2)}, u32[]{:S(2)}) collective-permute-start(f32[8,32,1,128]{3,1,0,2:T(8,128)S(1)} %get-tuple-element.112), channel_id=1, source_target_pairs={{1,0},{2,1},{3,2},{4,3},{5,4},{6,5},{7,6},{0,7},{9,8},{10,9},{11,1... | collective-permute-start | bytes 393224 | tf_op jit(solution)/shard_map/ppermute | solution.py:29
  244.0 3.4 %fusion.125 = f32[8,32,16,128]{3,1,0,2:T(8,128)S(1)} fusion(f32[8,32,1,128]{3,1,0,2:T(8,128)S(1)} %collective-permute-done.12, f32[8,32,16,128]{3,1,0,2:T(8,128)S(1)} %scatter-add.29, f32[8,32,1,128]{3,1,0,2:T(8,128)S(1)} %collective-permute-done.11, f32[8,32,16,127]{3,1,0,2:T(8,128)S(1)} %get-tuple-element.110, ...), kind=kOutput, calls=%fused_computation.132 | convolution fusion | flops 210763776 | bytes 10780672 | tf_op jit(solution)/shard_map/kab,rbky->raky/dot_general | solution.py:58
  247.4 2.0 slice_add_fusion
  249.4 2.5 copy.120
  (261 shorter events, 64.4 us)
Async XLA Ops:
  7.2 127.7 %all-reduce.21.cloned.1.call-start = ((), (), s32[]{:S(2)}) async-start(), calls=%async_computation | async-start | bytes 9437184 | tf_op jit(solution)/shard_map/psum | solution.py:11
  24.0 145.2 %collective-permute-start = (f32[8,32,1,128]{3,1,2,0:T(8,128)}, f32[8,32,1,128]{3,1,2,0:T(8,128)}, u32[]{:S(2)}, u32[]{:S(2)}) collective-permute-start(f32[8,32,1,128]{3,1,2,0:T(8,128)} %get-tuple-element.131), channel_id=1, source_target_pairs={{0,1},{1,2},{2,3},{3,4},{4,5},{5,6},{6,7},{7,0},{8,9},{9,10},{10,1... | collective-permute-start | bytes 393224 | tf_op jit(solution)/shard_map/ppermute | solution.py:26
  24.5 144.7 %collective-permute-start.2 = (f32[8,32,1,128]{3,1,2,0:T(8,128)}, f32[8,32,1,128]{3,1,2,0:T(8,128)}, u32[]{:S(2)}, u32[]{:S(2)}) collective-permute-start(f32[8,32,1,128]{3,1,2,0:T(8,128)} %get-tuple-element.132), channel_id=1, source_target_pairs={{1,0},{2,1},{3,2},{4,3},{5,4},{6,5},{7,6},{0,7},{9,8},{10,9},{11,1... | collective-permute-start | bytes 393224 | tf_op jit(solution)/shard_map/ppermute | solution.py:29
  137.6 30.3 %copy-start = (f32[6,32,15,128]{3,2,1,0:T(8,128)}, f32[6,32,15,128]{3,2,1,0:T(8,128)S(1)}, u32[]{:S(2)}) copy-start(f32[6,32,15,128]{3,2,1,0:T(8,128)S(1)} %slice_bitcast_fusion) | copy-start | bytes 4423684
  140.2 27.6 %collective-permute-start.1 = (f32[6,32,1,128]{3,1,0,2:T(8,128)S(1)}, f32[6,32,1,128]{3,1,0,2:T(8,128)S(1)}, u32[]{:S(2)}, u32[]{:S(2)}) collective-permute-start(f32[6,32,1,128]{3,1,0,2:T(8,128)S(1)} %bitcast.219), channel_id=1, source_target_pairs={{1,0},{2,1},{3,2},{4,3},{5,4},{6,5},{7,6},{0,7},{9,8},{10,9},{11,1... | collective-permute-start | bytes 294920 | tf_op jit(solution)/shard_map/ppermute | solution.py:17
  180.4 7.5 %collective-permute-start.3 = (f32[8,32,1,128]{3,1,0,2:T(8,128)S(1)}, f32[8,32,1,128]{3,1,0,2:T(8,128)S(1)}, u32[]{:S(2)}, u32[]{:S(2)}) collective-permute-start(f32[8,32,1,128]{3,1,0,2:T(8,128)S(1)} %get-tuple-element.127), channel_id=1, source_target_pairs={{0,1},{1,2},{2,3},{3,4},{4,5},{5,6},{6,7},{7,0},{8,9},{9,10},{10,1... | collective-permute-start | bytes 393224 | tf_op jit(solution)/shard_map/ppermute | solution.py:26
  180.5 7.5 %collective-permute-start.4 = (f32[8,32,1,128]{3,1,0,2:T(8,128)S(1)}, f32[8,32,1,128]{3,1,0,2:T(8,128)S(1)}, u32[]{:S(2)}, u32[]{:S(2)}) collective-permute-start(f32[8,32,1,128]{3,1,0,2:T(8,128)S(1)} %get-tuple-element.128), channel_id=1, source_target_pairs={{1,0},{2,1},{3,2},{4,3},{5,4},{6,5},{7,6},{0,7},{9,8},{10,9},{11,1... | collective-permute-start | bytes 393224 | tf_op jit(solution)/shard_map/ppermute | solution.py:29
  194.4 7.3 %collective-permute-start.5 = (f32[8,32,1,128]{3,1,0,2:T(8,128)S(1)}, f32[8,32,1,128]{3,1,0,2:T(8,128)S(1)}, u32[]{:S(2)}, u32[]{:S(2)}) collective-permute-start(f32[8,32,1,128]{3,1,0,2:T(8,128)S(1)} %get-tuple-element.123), channel_id=1, source_target_pairs={{0,1},{1,2},{2,3},{3,4},{4,5},{5,6},{6,7},{7,0},{8,9},{9,10},{10,1... | collective-permute-start | bytes 393224 | tf_op jit(solution)/shard_map/ppermute | solution.py:26
  194.6 7.1 %collective-permute-start.6 = (f32[8,32,1,128]{3,1,0,2:T(8,128)S(1)}, f32[8,32,1,128]{3,1,0,2:T(8,128)S(1)}, u32[]{:S(2)}, u32[]{:S(2)}) collective-permute-start(f32[8,32,1,128]{3,1,0,2:T(8,128)S(1)} %get-tuple-element.124), channel_id=1, source_target_pairs={{1,0},{2,1},{3,2},{4,3},{5,4},{6,5},{7,6},{0,7},{9,8},{10,9},{11,1... | collective-permute-start | bytes 393224 | tf_op jit(solution)/shard_map/ppermute | solution.py:29
  208.1 7.6 %collective-permute-start.7 = (f32[8,32,1,128]{3,1,0,2:T(8,128)S(1)}, f32[8,32,1,128]{3,1,0,2:T(8,128)S(1)}, u32[]{:S(2)}, u32[]{:S(2)}) collective-permute-start(f32[8,32,1,128]{3,1,0,2:T(8,128)S(1)} %get-tuple-element.119), channel_id=1, source_target_pairs={{0,1},{1,2},{2,3},{3,4},{4,5},{5,6},{6,7},{7,0},{8,9},{9,10},{10,1... | collective-permute-start | bytes 393224 | tf_op jit(solution)/shard_map/ppermute | solution.py:26
  208.2 7.5 %copy-start.30 = (f32[32,16,128]{2,0,1:T(8,128)S(1)}, f32[32,16,128]{2,0,1:T(8,128)}, u32[]{:S(2)}) copy-start(f32[32,16,128]{2,0,1:T(8,128)} %copy.102) | copy-start | bytes 786436
  208.2 7.5 %copy-start.31 = (f32[32,16,128]{2,0,1:T(8,128)S(1)}, f32[32,16,128]{2,0,1:T(8,128)}, u32[]{:S(2)}) copy-start(f32[32,16,128]{2,0,1:T(8,128)} %copy.103) | copy-start | bytes 786436
  208.2 7.5 %copy-start.32 = (f32[32,16,128]{2,0,1:T(8,128)S(1)}, f32[32,16,128]{2,0,1:T(8,128)}, u32[]{:S(2)}) copy-start(f32[32,16,128]{2,0,1:T(8,128)} %copy.101) | copy-start | bytes 786436
  208.2 7.5 %copy-start.33 = (f32[32,16,128]{2,0,1:T(8,128)S(1)}, f32[32,16,128]{2,0,1:T(8,128)}, u32[]{:S(2)}) copy-start(f32[32,16,128]{2,0,1:T(8,128)} %copy.100) | copy-start | bytes 786436
  208.2 7.5 %copy-start.34 = (f32[32,16,128]{2,0,1:T(8,128)S(1)}, f32[32,16,128]{2,0,1:T(8,128)}, u32[]{:S(2)}) copy-start(f32[32,16,128]{2,0,1:T(8,128)} %copy.96) | copy-start | bytes 786436
  208.3 7.5 %copy-start.35 = (f32[32,16,128]{2,0,1:T(8,128)S(1)}, f32[32,16,128]{2,0,1:T(8,128)}, u32[]{:S(2)}) copy-start(f32[32,16,128]{2,0,1:T(8,128)} %copy.97) | copy-start | bytes 786436
  208.3 7.5 %copy-start.48 = (f32[32,16,128]{2,0,1:T(8,128)S(1)}, f32[32,16,128]{2,0,1:T(8,128)}, u32[]{:S(2)}) copy-start(f32[32,16,128]{2,0,1:T(8,128)} %copy.98) | copy-start | bytes 786436
  208.3 7.5 %copy-start.49 = (f32[32,16,128]{2,0,1:T(8,128)S(1)}, f32[32,16,128]{2,0,1:T(8,128)}, u32[]{:S(2)}) copy-start(f32[32,16,128]{2,0,1:T(8,128)} %copy.99) | copy-start | bytes 786436
  208.3 7.5 %copy-start.57 = (f32[16,32,32]{2,1,0:T(8,128)S(1)}, f32[16,32,32]{2,1,0:T(8,128)}, u32[]{:S(2)}) copy-start(f32[16,32,32]{2,1,0:T(8,128)} %get-tuple-element.87) | copy-start | bytes 196612
  208.3 7.4 %collective-permute-start.8 = (f32[8,32,1,128]{3,1,0,2:T(8,128)S(1)}, f32[8,32,1,128]{3,1,0,2:T(8,128)S(1)}, u32[]{:S(2)}, u32[]{:S(2)}) collective-permute-start(f32[8,32,1,128]{3,1,0,2:T(8,128)S(1)} %get-tuple-element.120), channel_id=1, source_target_pairs={{1,0},{2,1},{3,2},{4,3},{5,4},{6,5},{7,6},{0,7},{9,8},{10,9},{11,1... | collective-permute-start | bytes 393224 | tf_op jit(solution)/shard_map/ppermute | solution.py:29
  222.2 5.1 %collective-permute-start.10 = (f32[8,32,1,128]{3,1,0,2:T(8,128)S(1)}, f32[8,32,1,128]{3,1,0,2:T(8,128)S(1)}, u32[]{:S(2)}, u32[]{:S(2)}) collective-permute-start(f32[8,32,1,128]{3,1,0,2:T(8,128)S(1)} %get-tuple-element.116), channel_id=1, source_target_pairs={{1,0},{2,1},{3,2},{4,3},{5,4},{6,5},{7,6},{0,7},{9,8},{10,9},{11,1... | collective-permute-start | bytes 393224 | tf_op jit(solution)/shard_map/ppermute | solution.py:29
  224.8 6.2 %collective-permute-start.9 = (f32[8,32,1,128]{3,1,0,2:T(8,128)S(1)}, f32[8,32,1,128]{3,1,0,2:T(8,128)S(1)}, u32[]{:S(2)}, u32[]{:S(2)}) collective-permute-start(f32[8,32,1,128]{3,1,0,2:T(8,128)S(1)} %get-tuple-element.115), channel_id=1, source_target_pairs={{0,1},{1,2},{2,3},{3,4},{4,5},{5,6},{6,7},{7,0},{8,9},{9,10},{10,1... | collective-permute-start | bytes 393224 | tf_op jit(solution)/shard_map/ppermute | solution.py:26
  237.5 6.2 %collective-permute-start.11 = (f32[8,32,1,128]{3,1,0,2:T(8,128)S(1)}, f32[8,32,1,128]{3,1,0,2:T(8,128)S(1)}, u32[]{:S(2)}, u32[]{:S(2)}) collective-permute-start(f32[8,32,1,128]{3,1,0,2:T(8,128)S(1)} %get-tuple-element.111), channel_id=1, source_target_pairs={{0,1},{1,2},{2,3},{3,4},{4,5},{5,6},{6,7},{7,0},{8,9},{9,10},{10,1... | collective-permute-start | bytes 393224 | tf_op jit(solution)/shard_map/ppermute | solution.py:26
  237.6 6.3 %collective-permute-start.12 = (f32[8,32,1,128]{3,1,0,2:T(8,128)S(1)}, f32[8,32,1,128]{3,1,0,2:T(8,128)S(1)}, u32[]{:S(2)}, u32[]{:S(2)}) collective-permute-start(f32[8,32,1,128]{3,1,0,2:T(8,128)S(1)} %get-tuple-element.112), channel_id=1, source_target_pairs={{1,0},{2,1},{3,2},{4,3},{5,4},{6,5},{7,6},{0,7},{9,8},{10,9},{11,1... | collective-permute-start | bytes 393224 | tf_op jit(solution)/shard_map/ppermute | solution.py:29
  (53 other events, 226.3 us)
Sparse Core Ops, SparseCore 0:
  19.2 115.5 all-reduce.20
where the time goes:
time: 264 us; the launch traced here: 260 us
  waiting for transfers between devices  117 us (44%)
  local copies, waits for them, and re-layouts  64.2 us (24%)
  starting transfers between devices  25.4 us (10%)
  matrix products  21.3 us (8%)
  between operations  19.5 us (7%)
  other arithmetic  12.6 us (5%)
    psum x1, waiting for transfers between devices, from_root(): return lax.psum(block, axis)  103 us
    ppermute x6, starting transfers between devices, padded_2(): lax.ppermute(lax.slice_in_dim(block, 0, width, axis=dim), axis, backward)  21.4 us
    dot_general x6, matrix products, advance(): jnp.einsum('kab,rbky->raky', mats, moved, precision=lax.Precision.HIGHEST...  21.3 us
    unnamed x137, local copies, waits for them, and re-layouts  17.6 us
    ppermute x6, waiting for transfers between devices, padded_2(): lax.ppermute(lax.slice_in_dim(block, block.shape[dim] - width, None, axis...  11.1 us
    scatter-add x6, local copies, waits for them, and re-layouts, inject(): return field.at[:, 0].add(hit.astype(jnp.float32))  8.81 us
    slice x6, local copies, waits for them, and re-layouts, advance(): centre[..., :-1]  6.41 us
  transfers between devices with their start and end apart: 14, of which 7 were waited for; matrix products, arithmetic and copies ran while one was open for 17% of the time, Pallas kernels for 0%

commit v1 on v0

--- a/solution.py
+++ b/solution.py
@@ -8,7 +8,7 @@
 
 def from_root(block, axis, owner):
     block = jnp.where(lax.axis_index(axis) == owner, block, jnp.zeros_like(block))
-    return lax.psum(block, axis)
+    return jnp.sum(lax.all_gather(block, axis), axis=0)
 
 
 def shifted(block, axis, distance):

time: 264 us -> 396 us (1.50)
  blocking collectives: 0 us -> 100 us
  other arithmetic: 12.6 us -> 29.7 us
  local copies, waits for them, and re-layouts: 64.2 us -> 72 us
    all_gather x0 -> x6, waiting for transfers between devices: none -> 104 us  [from_root(): return jnp.sum(lax.all_gather(block, axis), axis=0)]
    psum x1 -> x0, waiting for transfers between devices: 103 us -> none  [from_root(): return lax.psum(block, axis)]
    all_gather x0 -> x6, blocking collectives: none -> 100 us  [from_root(): return jnp.sum(lax.all_gather(block, axis), axis=0)]
    reduce_sum x0 -> x12, other arithmetic: none -> 18.9 us  [from_root(): return jnp.sum(lax.all_gather(block, axis), axis=0)]
    unnamed x137 -> x135, local copies, waits for them, and re-layouts: 17.6 us -> 20.4 us
  transfers between devices with their start and end apart: 14 -> 19, of which waited for: 7 -> 10; matrix products, arithmetic and copies ran while one was open for 17% -> 19% of each run, Pallas kernels for 0% -> 0%
where the time goes in v1:
time: 396 us; the launch traced here: 388 us
  waiting for transfers between devices  120 us (30%)
  blocking collectives  100 us (25%)
  local copies, waits for them, and re-layouts  72 us (18%)
  other arithmetic  29.7 us (8%)
  starting transfers between devices  25.6 us (6%)
  matrix products  21.3 us (5%)
  between operations  19.7 us (5%)
    all_gather x6, waiting for transfers between devices, from_root(): return jnp.sum(lax.all_gather(block, axis), axis=0)  104 us
    all_gather x6, blocking collectives, from_root(): return jnp.sum(lax.all_gather(block, axis), axis=0)  100 us
    ppermute x6, starting transfers between devices, padded_2(): lax.ppermute(lax.slice_in_dim(block, 0, width, axis=dim), axis, backward)  21.4 us
    dot_general x6, matrix products, advance(): jnp.einsum('kab,rbky->raky', mats, moved, precision=lax.Precision.HIGHEST...  21.3 us
    unnamed x135, local copies, waits for them, and re-layouts  20.4 us
    reduce_sum x12, other arithmetic, from_root(): return jnp.sum(lax.all_gather(block, axis), axis=0)  18.9 us
    ppermute x6, waiting for transfers between devices, padded_2(): lax.ppermute(lax.slice_in_dim(block, block.shape[dim] - width, None, axis...  11.1 us
    scatter-add x6, local copies, waits for them, and re-layouts, inject(): return field.at[:, 0].add(hit.astype(jnp.float32))  8.81 us
  transfers between devices with their start and end apart: 19, of which 10 were waited for; matrix products, arithmetic and copies ran while one was open for 19% of the time, Pallas kernels for 0%

profile of v1, /device:TPU:0, one launch (start us, length us, event | category | flops | bytes accessed | tf_op | source)
XLA Modules:
  0.0 388.5 jit_solution(6470135423721536068)
XLA Ops:
  12.6 3.5 slice_select_fusion
  24.8 4.0 %collective-permute-start.2 = (f32[8,32,1,128]{3,1,2,0:T(8,128)}, f32[8,32,1,128]{3,1,2,0:T(8,128)}, u32[]{:S(2)}, u32[]{:S(2)}) collective-permute-start(f32[8,32,1,128]{3,1,2,0:T(8,128)} %get-tuple-element.121), channel_id=1, source_target_pairs={{1,0},{2,1},{3,2},{4,3},{5,4},{6,5},{7,6},{0,7},{9,8},{10,9},{11,1... | collective-permute-start | bytes 393224 | tf_op jit(solution)/shard_map/ppermute | solution.py:29
  29.8 15.3 %all-gather.6 = f32[4,16,32,32]{3,2,1,0:T(8,128)S(1)} all-gather(f32[1,16,32,32]{3,2,1,0:T(8,128)S(1)} %get-tuple-element.148), channel_id=8, replica_groups=mesh['rcp'=4,'lon'=8] {'rcp'}, dimensions={0}, use_global_device_ids=true | all-gather | bytes 327680 | tf_op jit(solution)/shard_map/all_gather | solution.py:11
  45.9 19.0 %all-gather.7 = f32[4,16,32,32]{3,2,1,0:T(8,128)S(1)} all-gather(f32[1,16,32,32]{3,2,1,0:T(8,128)} %get-tuple-element.147), channel_id=9, replica_groups=mesh['rcp'=4,'lon'=8] {'rcp'}, dimensions={0}, use_global_device_ids=true | all-gather | bytes 327680 | tf_op jit(solution)/shard_map/all_gather | solution.py:11
  65.7 17.9 %all-gather.8 = f32[4,16,32,32]{3,2,1,0:T(8,128)S(1)} all-gather(f32[1,16,32,32]{3,2,1,0:T(8,128)} %get-tuple-element.146), channel_id=10, replica_groups=mesh['rcp'=4,'lon'=8] {'rcp'}, dimensions={0}, use_global_device_ids=true | all-gather | bytes 327680 | tf_op jit(solution)/shard_map/all_gather | solution.py:11
  84.4 20.5 %all-gather.9 = f32[4,16,32,32]{3,2,1,0:T(8,128)S(1)} all-gather(f32[1,16,32,32]{3,2,1,0:T(8,128)} %get-tuple-element.145), channel_id=11, replica_groups=mesh['rcp'=4,'lon'=8] {'rcp'}, dimensions={0}, use_global_device_ids=true | all-gather | bytes 327680 | tf_op jit(solution)/shard_map/all_gather | solution.py:11
  105.8 12.9 %all-gather.10 = f32[4,16,32,32]{3,2,1,0:T(8,128)S(1)} all-gather(f32[1,16,32,32]{3,2,1,0:T(8,128)} %get-tuple-element.149), channel_id=12, replica_groups=mesh['rcp'=4,'lon'=8] {'rcp'}, dimensions={0}, use_global_device_ids=true | all-gather | bytes 327680 | tf_op jit(solution)/shard_map/all_gather | solution.py:11
  119.5 14.8 %all-gather.11 = f32[4,16,32,32]{3,2,1,0:T(8,128)S(1)} all-gather(f32[1,16,32,32]{3,2,1,0:T(8,128)S(1)} %get-tuple-element.144), channel_id=13, replica_groups=mesh['rcp'=4,'lon'=8] {'rcp'}, dimensions={0}, use_global_device_ids=true | all-gather | bytes 327680 | tf_op jit(solution)/shard_map/all_gather | solution.py:11
  143.1 5.5 %all-gather.23.cloned.1.call-done = f32[4,2,1,32,16,128]{5,4,3,2,1,0:T(8,128)} async-done(((f32[1,2,1,32,16,128]{5,4,3,2,1,0:T(8,128)}), f32[4,2,1,32,16,128]{5,4,3,2,1,0:T(8,128)}) %all-gather.23.cloned.1.call-update) | async-done | bytes 2097168 | tf_op jit(solution)/shard_map/all_gather | solution.py:11
  151.2 34.3 %all-gather.25.cloned.1.call-done = f32[4,2,1,32,16,128]{5,4,3,2,1,0:T(8,128)} async-done(((f32[1,2,1,32,16,128]{5,4,3,2,1,0:T(8,128)}), f32[4,2,1,32,16,128]{5,4,3,2,1,0:T(8,128)}) %all-gather.25.cloned.1.call-update) | async-done | bytes 2097168 | tf_op jit(solution)/shard_map/all_gather | solution.py:11
  187.3 35.1 %all-gather.27.cloned.1.call-done = f32[4,2,1,32,16,128]{5,4,3,2,1,0:T(8,128)} async-done(((f32[1,2,1,32,16,128]{5,4,3,2,1,0:T(8,128)}), f32[4,2,1,32,16,128]{5,4,3,2,1,0:T(8,128)}) %all-gather.27.cloned.1.call-update) | async-done | bytes 2097168 | tf_op jit(solution)/shard_map/all_gather | solution.py:11
  230.5 28.8 %all-gather.29.cloned.1.call-done = f32[4,2,1,32,16,128]{5,4,3,2,1,0:T(8,128)} async-done(((f32[1,2,1,32,16,128]{5,4,3,2,1,0:T(8,128)}), f32[4,2,1,32,16,128]{5,4,3,2,1,0:T(8,128)}) %all-gather.29.cloned.1.call-update) | async-done | bytes 2097168 | tf_op jit(solution)/shard_map/all_gather | solution.py:11
  268.8 3.2 collective-permute-start.1
  299.0 4.4 %fusion.73 = f32[16,8,128,32]{2,3,1,0:T(8,128)S(1)} fusion(f32[16,32,32]{2,1,0:T(8,128)S(1)} %copy-done.22, f32[8,32,1,128]{3,1,2,0:T(8,128)} %collective-permute-done.2, f32[8,32,16,128]{3,1,2,0:T(8,128)S(1)} %scatter-add.20, f32[8,32,1,128]{3,1,2,0:T(8,128)} %collective-permute-done, f32[8,32,16,127]{3,1,2,0:T(8,128)S(1)} %copy-done.13, ...), kind=kOutput, calls=%fused_computation.80 | convolution fusion | flops 210763776 | bytes 10780672 | tf_op jit(solution)/shard_map/kab,rbky->raky/dot_general | solution.py:58
  309.0 3.7 collective-permute-start.4
  316.6 3.4 fusion.57
  323.2 3.6 collective-permute-start.6
  330.4 3.4 fusion.44
  336.9 3.8 collective-permute-start.8
  344.4 3.4 fusion.31
  356.0 3.8 collective-permute-done.9
  359.8 3.4 fusion.18
  366.3 3.8 collective-permute-start.12
  372.6 3.4 fusion.125
  (294 shorter events, 114.0 us)
Async XLA Ops:
  7.2 130.7 %all-gather.19.cloned.1.call-start = ((), (), s32[]{:S(2)}) async-start(), calls=%async_computation | async-start | bytes 2621440 | tf_op jit(solution)/shard_map/all_gather | solution.py:11
  16.1 124.3 %all-gather.21.cloned.1.call-start = ((), (), s32[]{:S(2)}) async-start(), calls=%async_computation.1 | async-start | bytes 2621440 | tf_op jit(solution)/shard_map/all_gather | solution.py:11
  16.9 131.7 %all-gather.23.cloned.1.call-start = ((), (), s32[]{:S(2)}) async-start(), calls=%async_computation.2 | async-start | bytes 2621440 | tf_op jit(solution)/shard_map/all_gather | solution.py:11
  17.6 167.9 %all-gather.25.cloned.1.call-start = ((), (), s32[]{:S(2)}) async-start(), calls=%async_computation.3 | async-start | bytes 2621440 | tf_op jit(solution)/shard_map/all_gather | solution.py:11
  18.2 204.2 %all-gather.27.cloned.1.call-start = ((), (), s32[]{:S(2)}) async-start(), calls=%async_computation.4 | async-start | bytes 2621440 | tf_op jit(solution)/shard_map/all_gather | solution.py:11
  18.8 240.5 %all-gather.29.cloned.1.call-start = ((), (), s32[]{:S(2)}) async-start(), calls=%async_computation.5 | async-start | bytes 2621440 | tf_op jit(solution)/shard_map/all_gather | solution.py:11
  19.4 9.4 %copy-start.57 = (f32[1,16,32,32]{3,2,1,0:T(8,128)S(1)}, f32[1,16,32,32]{3,2,1,0:T(8,128)}, u32[]{:S(2)}) copy-start(f32[1,16,32,32]{3,2,1,0:T(8,128)} %param.21) | copy-start | bytes 196612
  24.3 273.5 %collective-permute-start = (f32[8,32,1,128]{3,1,2,0:T(8,128)}, f32[8,32,1,128]{3,1,2,0:T(8,128)}, u32[]{:S(2)}, u32[]{:S(2)}) collective-permute-start(f32[8,32,1,128]{3,1,2,0:T(8,128)} %get-tuple-element.120), channel_id=1, source_target_pairs={{0,1},{1,2},{2,3},{3,4},{4,5},{5,6},{6,7},{7,0},{8,9},{9,10},{10,1... | collective-permute-start | bytes 393224 | tf_op jit(solution)/shard_map/ppermute | solution.py:26
  24.8 273.1 %collective-permute-start.2 = (f32[8,32,1,128]{3,1,2,0:T(8,128)}, f32[8,32,1,128]{3,1,2,0:T(8,128)}, u32[]{:S(2)}, u32[]{:S(2)}) collective-permute-start(f32[8,32,1,128]{3,1,2,0:T(8,128)} %get-tuple-element.121), channel_id=1, source_target_pairs={{1,0},{2,1},{3,2},{4,3},{5,4},{6,5},{7,6},{0,7},{9,8},{10,9},{11,1... | collective-permute-start | bytes 393224 | tf_op jit(solution)/shard_map/ppermute | solution.py:29
  265.5 30.9 %copy-start = (f32[6,32,15,128]{3,2,1,0:T(8,128)}, f32[6,32,15,128]{3,2,1,0:T(8,128)S(1)}, u32[]{:S(2)}) copy-start(f32[6,32,15,128]{3,2,1,0:T(8,128)S(1)} %slice_bitcast_fusion) | copy-start | bytes 4423684
  268.8 27.6 %collective-permute-start.1 = (f32[6,32,1,128]{3,1,0,2:T(8,128)S(1)}, f32[6,32,1,128]{3,1,0,2:T(8,128)S(1)}, u32[]{:S(2)}, u32[]{:S(2)}) collective-permute-start(f32[6,32,1,128]{3,1,0,2:T(8,128)S(1)} %bitcast.189), channel_id=1, source_target_pairs={{1,0},{2,1},{3,2},{4,3},{5,4},{6,5},{7,6},{0,7},{9,8},{10,9},{11,1... | collective-permute-start | bytes 294920 | tf_op jit(solution)/shard_map/ppermute | solution.py:17
  309.0 7.5 %collective-permute-start.3 = (f32[8,32,1,128]{3,1,0,2:T(8,128)S(1)}, f32[8,32,1,128]{3,1,0,2:T(8,128)S(1)}, u32[]{:S(2)}, u32[]{:S(2)}) collective-permute-start(f32[8,32,1,128]{3,1,0,2:T(8,128)S(1)} %get-tuple-element.116), channel_id=1, source_target_pairs={{0,1},{1,2},{2,3},{3,4},{4,5},{5,6},{6,7},{7,0},{8,9},{9,10},{10,1... | collective-permute-start | bytes 393224 | tf_op jit(solution)/shard_map/ppermute | solution.py:26
  309.0 7.5 %collective-permute-start.4 = (f32[8,32,1,128]{3,1,0,2:T(8,128)S(1)}, f32[8,32,1,128]{3,1,0,2:T(8,128)S(1)}, u32[]{:S(2)}, u32[]{:S(2)}) collective-permute-start(f32[8,32,1,128]{3,1,0,2:T(8,128)S(1)} %get-tuple-element.117), channel_id=1, source_target_pairs={{1,0},{2,1},{3,2},{4,3},{5,4},{6,5},{7,6},{0,7},{9,8},{10,9},{11,1... | collective-permute-start | bytes 393224 | tf_op jit(solution)/shard_map/ppermute | solution.py:29
  323.0 7.3 %collective-permute-start.5 = (f32[8,32,1,128]{3,1,0,2:T(8,128)S(1)}, f32[8,32,1,128]{3,1,0,2:T(8,128)S(1)}, u32[]{:S(2)}, u32[]{:S(2)}) collective-permute-start(f32[8,32,1,128]{3,1,0,2:T(8,128)S(1)} %get-tuple-element.112), channel_id=1, source_target_pairs={{0,1},{1,2},{2,3},{3,4},{4,5},{5,6},{6,7},{7,0},{8,9},{9,10},{10,1... | collective-permute-start | bytes 393224 | tf_op jit(solution)/shard_map/ppermute | solution.py:26
  323.2 7.1 %collective-permute-start.6 = (f32[8,32,1,128]{3,1,0,2:T(8,128)S(1)}, f32[8,32,1,128]{3,1,0,2:T(8,128)S(1)}, u32[]{:S(2)}, u32[]{:S(2)}) collective-permute-start(f32[8,32,1,128]{3,1,0,2:T(8,128)S(1)} %get-tuple-element.113), channel_id=1, source_target_pairs={{1,0},{2,1},{3,2},{4,3},{5,4},{6,5},{7,6},{0,7},{9,8},{10,9},{11,1... | collective-permute-start | bytes 393224 | tf_op jit(solution)/shard_map/ppermute | solution.py:29
  336.7 7.6 %collective-permute-start.7 = (f32[8,32,1,128]{3,1,0,2:T(8,128)S(1)}, f32[8,32,1,128]{3,1,0,2:T(8,128)S(1)}, u32[]{:S(2)}, u32[]{:S(2)}) collective-permute-start(f32[8,32,1,128]{3,1,0,2:T(8,128)S(1)} %get-tuple-element.108), channel_id=1, source_target_pairs={{0,1},{1,2},{2,3},{3,4},{4,5},{5,6},{6,7},{7,0},{8,9},{9,10},{10,1... | collective-permute-start | bytes 393224 | tf_op jit(solution)/shard_map/ppermute | solution.py:26
  336.8 7.5 %copy-start.19 = (f32[16,32,32]{2,1,0:T(8,128)S(1)}, f32[16,32,32]{2,1,0:T(8,128)}, u32[]{:S(2)}) copy-start(f32[16,32,32]{2,1,0:T(8,128)} %reduce.33) | copy-start | bytes 196612
  336.8 7.5 %copy-start.35 = (f32[32,16,128]{2,0,1:T(8,128)S(1)}, f32[32,16,128]{2,0,1:T(8,128)}, u32[]{:S(2)}) copy-start(f32[32,16,128]{2,0,1:T(8,128)} %copy.58) | copy-start | bytes 786436
  336.8 7.5 %copy-start.36 = (f32[32,16,128]{2,0,1:T(8,128)S(1)}, f32[32,16,128]{2,0,1:T(8,128)}, u32[]{:S(2)}) copy-start(f32[32,16,128]{2,0,1:T(8,128)} %copy.59) | copy-start | bytes 786436
  336.9 7.4 %collective-permute-start.8 = (f32[8,32,1,128]{3,1,0,2:T(8,128)S(1)}, f32[8,32,1,128]{3,1,0,2:T(8,128)S(1)}, u32[]{:S(2)}, u32[]{:S(2)}) collective-permute-start(f32[8,32,1,128]{3,1,0,2:T(8,128)S(1)} %get-tuple-element.109), channel_id=1, source_target_pairs={{1,0},{2,1},{3,2},{4,3},{5,4},{6,5},{7,6},{0,7},{9,8},{10,9},{11,1... | collective-permute-start | bytes 393224 | tf_op jit(solution)/shard_map/ppermute | solution.py:29
  350.8 5.1 %collective-permute-start.10 = (f32[8,32,1,128]{3,1,0,2:T(8,128)S(1)}, f32[8,32,1,128]{3,1,0,2:T(8,128)S(1)}, u32[]{:S(2)}, u32[]{:S(2)}) collective-permute-start(f32[8,32,1,128]{3,1,0,2:T(8,128)S(1)} %get-tuple-element.105), channel_id=1, source_target_pairs={{1,0},{2,1},{3,2},{4,3},{5,4},{6,5},{7,6},{0,7},{9,8},{10,9},{11,1... | collective-permute-start | bytes 393224 | tf_op jit(solution)/shard_map/ppermute | solution.py:29
  353.5 6.2 %collective-permute-start.9 = (f32[8,32,1,128]{3,1,0,2:T(8,128)S(1)}, f32[8,32,1,128]{3,1,0,2:T(8,128)S(1)}, u32[]{:S(2)}, u32[]{:S(2)}) collective-permute-start(f32[8,32,1,128]{3,1,0,2:T(8,128)S(1)} %get-tuple-element.104), channel_id=1, source_target_pairs={{0,1},{1,2},{2,3},{3,4},{4,5},{5,6},{6,7},{7,0},{8,9},{9,10},{10,1... | collective-permute-start | bytes 393224 | tf_op jit(solution)/shard_map/ppermute | solution.py:26
  366.1 6.2 %collective-permute-start.11 = (f32[8,32,1,128]{3,1,0,2:T(8,128)S(1)}, f32[8,32,1,128]{3,1,0,2:T(8,128)S(1)}, u32[]{:S(2)}, u32[]{:S(2)}) collective-permute-start(f32[8,32,1,128]{3,1,0,2:T(8,128)S(1)} %get-tuple-element.100), channel_id=1, source_target_pairs={{0,1},{1,2},{2,3},{3,4},{4,5},{5,6},{6,7},{7,0},{8,9},{9,10},{10,1... | collective-permute-start | bytes 393224 | tf_op jit(solution)/shard_map/ppermute | solution.py:26
  366.3 6.3 %collective-permute-start.12 = (f32[8,32,1,128]{3,1,0,2:T(8,128)S(1)}, f32[8,32,1,128]{3,1,0,2:T(8,128)S(1)}, u32[]{:S(2)}, u32[]{:S(2)}) collective-permute-start(f32[8,32,1,128]{3,1,0,2:T(8,128)S(1)} %get-tuple-element.101), channel_id=1, source_target_pairs={{1,0},{2,1},{3,2},{4,3},{5,4},{6,5},{7,6},{0,7},{9,8},{10,9},{11,1... | collective-permute-start | bytes 393224 | tf_op jit(solution)/shard_map/ppermute | solution.py:29
  (57 other events, 282.4 us)
Sparse Core Ops, SparseCore 0:
  16.2 46.0 all-gather.18
  64.2 45.1 all-gather.20
  111.3 37.2 all-gather.22
  150.3 35.1 all-gather.24
  187.2 35.1 all-gather.26
  224.1 35.1 all-gather.28
